TPU v7x, 32 devices: a whole 2x2x4 slice. The times are simulated.
32 devices in a mesh: users: 8 (over z, y), seq: 4 (over x, core).
Axes of the slice: x: 2, y: 2, z: 4, core: 2. Of those that a mesh axis runs over, the one named last changes fastest.
Arguments:
- raw_events: bfloat16 [4, 3072, 512], P('seq', 'users'), may hold values from -6 to 6
- target_user: int32 [4, 3072], P('seq', 'users'), may hold values from 0 to 7, as said below
- target_place: int32 [4, 3072], P('seq', 'users'), may hold values from 0 to 1023, as said below
- send_counts: int32 [4, 8, 8], P('seq', 'users'), may hold values from 0 to 48, as said below
- lengths: int32 [8], P('users'), may hold values from 512 to 1024, as said below
- cotangent: bfloat16 [8, 1024, 512], P('users', 'seq'), may hold values from -0.06591797 to 0.06591797
- encoder_in: bfloat16 [512, 512], replicated, may hold values from -0.25 to 0.25
- encoder_out: bfloat16 [512, 512], replicated, may hold values from -0.25 to 0.25
- proj_weight: bfloat16 [512, 1024], replicated, may hold values from -0.25 to 0.25
- proj_bias: float32 [1024], replicated, may hold values from -3 to 3
- out_weight: bfloat16 [256, 512], replicated, may hold values from -0.375 to 0.375
- out_bias: float32 [512], replicated, may hold values from -3 to 3
Outputs:
- layer_out: bfloat16 [8, 1024, 512], P('users', 'seq')
- grad_proj_weight: bfloat16 [512, 1024], replicated
- grad_proj_bias: float32 [1024], replicated
- grad_out_weight: bfloat16 [256, 512], replicated
- grad_out_bias: float32 [512], replicated
Inputs may be any that keep to these rules, and one draw needn't show every extreme that they name: `target_user`: within one ingestion shard the event rows come first, grouped by user in increasing order; the rows after the shard's total of send_counts carry no event. An event of block b has a position in b * 256 to (b + 1) * 256 - 1. The events of a user are exactly its positions 0 to its length - 1, each once. `target_place`: see target_user. send_counts[b, i, u] rows of shard i in block b go to user u; at most 48, and exactly 48 for some shard and user. The counts of a user in block b sum to min(max(length - b * 256, 0), 256). `lengths`: some user has length exactly 1024.
All inputs are finite; a program needn't handle non-finite values.
Results may differ from a plain program's by a relative error of at most 0.0084.
The roundings to bfloat16 on the way count: a program that leaves them out, or rounds other values in their place, can miss the bound.
Values may be sent and summed in bfloat16 or wider, within the bound.
A program may use at most 64 MiB of HBM per device.

v0:
```python
import functools

import jax
import jax.numpy as jnp
from jax import lax
from jax.experimental import pallas as pl
from jax.experimental.pallas import tpu as pltpu
from jax.sharding import PartitionSpec as P

HEAD = 64
EPSILON = 1e-05
LANES = 128
ROWS = 16
F32 = jnp.float32
BF16 = jnp.bfloat16


def sigmoid(values):
    return 0.5 * jnp.tanh(0.5 * values) + 0.5


def silu(values):
    return values * sigmoid(values)


def silu_grad(values):
    gate = sigmoid(values)
    return gate * (1.0 + values * (1.0 - gate))


def layer_norm(values):
    center = values - jnp.mean(values, axis=-1, keepdims=True)
    inverse = lax.rsqrt(jnp.mean(center * center, axis=-1, keepdims=True) + EPSILON)
    return center * inverse, inverse


def dot(a, b, contract=(1, 0)):
    return lax.dot_general(
        a, b, (((contract[0],), (contract[1],)), ((), ())), preferred_element_type=F32
    )


def flip(index, bit):
    return index + bit * (1 - 2 * ((index // bit) % 2))


def flip_all(index, delta):
    bit = 1
    while bit <= delta:
        if delta & bit:
            index = flip(index, bit)
        bit *= 2
    return index


def plan_of(users, seqs, groups):
    bits = []
    for axis, size in (("seq", seqs), ("users", users)):
        bit = 1
        while bit < size:
            bits.append((axis, bit))
            bit *= 2
    head, rest = bits[:1], bits[1:]
    turn, tail = rest[:3], rest[3:]
    devices = users * seqs
    plans = []
    base = 0
    for chunks, most in groups:
        each = -(-chunks // devices)
        streams = []
        for i in range(most):
            share = (each + most - 1 - i) // most
            if share == 0:
                continue
            k = i % 3
            order = head + turn[k:] + turn[:k] + tail
            streams.append((base, share * devices, order))
            base += share * devices
        plans.append(streams)
    return plans, len(bits), base


def groups_of(model, width):
    tile = ROWS * LANES
    return (2 * model * width // tile, 3), (3 * model * width // tile, 6)


def kernel(
    users,
    seqs,
    raw_hbm,
    user_ref,
    place_ref,
    counts_ref,
    length_ref,
    cot_hbm,
    enc_in_hbm,
    enc_out_hbm,
    proj_w_hbm,
    proj_b_ref,
    out_w_hbm,
    out_b_ref,
    layer_ref,
    full,
    bias_ref,
    send_buf,
    recv_buf,
    spot_out,
    spot_in,
    seq_sc,
    norm_sc,
    proj_sc,
    gate_sc,
    kv,
    qb,
    gb,
    w_sc,
    s_sc,
    att,
    dq,
    dk,
    dv,
    dproj,
    work,
    landing,
    bias,
    bias_in,
    a2a_send,
    a2a_recv,
    spot_send,
    spot_recv,
    kv_send,
    kv_recv,
    q_send,
    q_recv,
    g_send,
    g_recv,
    rs_send,
    rs_recv,
    ag_send,
    ag_recv,
    b_send,
    b_recv,
    raw_ref,
    cot_ref,
    enc_in_ref,
    enc_out_ref,
    proj_w_ref,
    out_w_ref,
    in_sem,
):
    me_u = lax.axis_index("users")
    me_s = lax.axis_index("seq")
    MESH = pl.DeviceIdType.MESH
    slots, model = raw_ref.shape
    block = cot_ref.shape[0]
    width = out_w_ref.shape[0]
    pairs = width // LANES
    capacity = slots // users
    cap_pad = send_buf.shape[1]
    scale = HEAD ** (-0.5)

    barrier = pltpu.get_barrier_semaphore()
    for delta in range(1, users):
        pl.semaphore_signal(
            barrier,
            inc=1,
            device_id=(lax.rem(me_u + delta, users), me_s),
            device_id_type=MESH,
        )
    for delta in range(1, seqs):
        pl.semaphore_signal(
            barrier,
            inc=1,
            device_id=(me_u, lax.rem(me_s + delta, seqs)),
            device_id_type=MESH,
        )

    loads = [
        pltpu.make_async_copy(source, target, in_sem.at[i])
        for i, (source, target) in enumerate(
            (
                (raw_hbm, raw_ref),
                (enc_in_hbm, enc_in_ref),
                (enc_out_hbm, enc_out_ref),
                (cot_hbm, cot_ref),
                (proj_w_hbm, proj_w_ref),
                (out_w_hbm, out_w_ref),
            )
        )
    ]
    for load in loads:
        load.start()

    loads[0].wait()
    loads[1].wait()
    loads[2].wait()
    hidden = silu(dot(raw_ref[...], enc_in_ref[...])).astype(BF16)
    encoded = dot(hidden, enc_out_ref[...]).astype(BF16)
    target = user_ref[...]
    lane_row = lax.broadcasted_iota(jnp.int32, (1, slots), 1)
    first = jnp.zeros((1, slots), jnp.int32)
    total = jnp.int32(0)
    for u in range(users):
        first = jnp.where(target == u, total, first)
        total = total + counts_ref[0, u]
    flat = jnp.where(lane_row < total, target * cap_pad + lane_row - first, -1)
    hot = lax.broadcasted_iota(jnp.int32, (users * cap_pad, slots), 0) == flat
    bucket = dot(hot.astype(F32).astype(BF16), encoded).astype(BF16)
    local_place = (place_ref[...] - me_s * block + 1).astype(F32)
    spots = jnp.sum(jnp.where(hot, local_place, 0.0), axis=1, keepdims=True) - 1.0
    diagonal = lax.broadcasted_iota(
        jnp.int32, (users, cap_pad, LANES), 1
    ) == lax.broadcasted_iota(jnp.int32, (users, cap_pad, LANES), 2)
    send_buf[...] = bucket.reshape(users, cap_pad, model)
    spot_out[...] = jnp.sum(
        jnp.where(diagonal, spots.reshape(users, cap_pad, 1), 0.0), axis=1, keepdims=True
    )

    pl.semaphore_wait(barrier, users - 1 + seqs - 1)

    sends = []
    for delta in range(1, users):
        peer = lax.rem(me_u + delta, users)
        copy = pltpu.make_async_remote_copy(
            src_ref=send_buf.at[peer],
            dst_ref=recv_buf.at[me_u],
            send_sem=a2a_send.at[delta],
            recv_sem=a2a_recv.at[delta],
            device_id=(peer, me_s),
            device_id_type=MESH,
        )
        spot_copy = pltpu.make_async_remote_copy(
            src_ref=spot_out.at[peer],
            dst_ref=spot_in.at[me_u],
            send_sem=spot_send.at[delta],
            recv_sem=spot_recv.at[delta],
            device_id=(peer, me_s),
            device_id_type=MESH,
        )
        spot_copy.start()
        copy.start()
        sends.append(spot_copy)
        sends.append(copy)
    recv_buf[me_u] = send_buf[me_u]
    spot_in[me_u] = spot_out[me_u]
    length = length_ref[0]
    rows = lax.broadcasted_iota(jnp.int32, (block, 1), 0)
    present = me_s * block + rows < length
    loads[3].wait()
    loads[4].wait()
    loads[5].wait()
    d_out = jnp.where(present, cot_ref[...], jnp.zeros((block, model), BF16))
    for copy in sends:
        copy.wait()
    arrived = recv_buf[...].reshape(users * cap_pad, model)
    where_to = jnp.sum(jnp.where(diagonal, spot_in[...], 0.0), axis=2, keepdims=True)
    where_to = where_to.reshape(users * cap_pad, 1).astype(jnp.int32)
    placed = (
        lax.broadcasted_iota(jnp.int32, (users * cap_pad, block), 1) == where_to
    ).astype(F32).astype(BF16)
    sequence = dot(placed, arrived, (0, 0))
    seq_sc[...] = sequence.astype(BF16)
    normed = layer_norm(sequence)[0].astype(BF16)
    norm_sc[...] = normed
    projected = dot(normed, proj_w_ref[...]) + proj_b_ref[...]
    proj_sc[...] = projected
    gates = silu(projected).astype(BF16)
    gate_sc[...] = gates[:, :width]
    for p in range(pairs):
        low = p * LANES
        kv[me_s, p] = gates[:, 3 * width + low : 3 * width + low + LANES]
        kv[me_s, pairs + p] = gates[:, width + low : width + low + LANES]
        qb[me_s, p] = gates[:, 2 * width + low : 2 * width + low + LANES]

    steps = []
    bit = seqs // 2
    while bit >= 1:
        steps.append(bit)
        bit //= 2
    moves = []
    held = [0]
    for bit in steps:
        for delta in held:
            moves.append((delta, bit))
        held = held + [delta + bit for delta in held]

    def move(buf, send_sem, recv_sem, index):
        delta, bit = moves[index]
        held_block = flip_all(me_s, delta)
        peer = flip(me_s, bit)
        return (
            held_block,
            peer,
            pltpu.make_async_remote_copy(
                src_ref=buf.at[held_block],
                dst_ref=buf.at[held_block],
                send_sem=send_sem.at[index],
                recv_sem=recv_sem.at[delta + bit],
                device_id=(me_u, peer),
                device_id_type=MESH,
            ),
        )

    def arrive(buf, send_sem, recv_sem, delta):
        low_bit = delta & -delta
        source = flip_all(me_s, delta)
        pltpu.make_async_remote_copy(
            src_ref=buf.at[source],
            dst_ref=buf.at[source],
            send_sem=send_sem.at[0],
            recv_sem=recv_sem.at[delta],
            device_id=(me_u, flip(me_s, low_bit)),
            device_id_type=MESH,
        ).wait_recv()

    def up(held_block, peer):
        return held_block < peer

    def down(held_block, peer):
        return held_block > peer

    def start_own(buf, send_sem, recv_sem, way):
        for index, (delta, bit) in enumerate(moves):
            if delta == 0:
                held_block, peer, copy = move(buf, send_sem, recv_sem, index)

                @pl.when(way(held_block, peer))
                def _():
                    copy.start()

    def take(buf, send_sem, recv_sem, way, delta):
        source = flip_all(me_s, delta)

        @pl.when(way(source, me_s))
        def _():
            arrive(buf, send_sem, recv_sem, delta)
            for index, (held_delta, bit) in enumerate(moves):
                if held_delta == delta:
                    move(buf, send_sem, recv_sem, index)[2].start()

    def finish(buf, send_sem, recv_sem, way):
        for index in range(len(moves)):
            held_block, peer, copy = move(buf, send_sem, recv_sem, index)

            @pl.when(way(held_block, peer))
            def _():
                copy.wait_send()

    kv_set = (kv, kv_send, kv_recv, up)
    q_set = (qb, q_send, q_recv, down)
    g_set = (gb, g_send, g_recv, down)
    start_own(*kv_set)
    start_own(*q_set)

    lane_is_low = lax.broadcasted_iota(jnp.int32, (block, LANES), 1) < HEAD

    def half_of(values, hh):
        zero = jnp.zeros_like(values)
        return jnp.where(lane_is_low, values, zero) if hh == 0 else jnp.where(lane_is_low, zero, values)

    def scores_of(delta):
        other = flip_all(me_s, delta)
        q_index = jnp.maximum(other, me_s)
        k_index = jnp.minimum(other, me_s)
        bound = jnp.minimum(q_index * block + rows, length - 1) - k_index * block
        allowed = lax.broadcasted_iota(jnp.int32, (block, block), 1) <= bound
        for p in range(pairs):
            queries = qb[q_index, p]
            keys = kv[k_index, p]
            for hh in range(2):
                score = dot(half_of(queries, hh), keys, (1, 1)) * scale
                gate = sigmoid(score)
                plain = score * gate
                w_sc[delta, p, hh] = jnp.where(allowed, plain, 0.0).astype(BF16)
                s_sc[delta, p, hh] = jnp.where(allowed, gate + plain * (1.0 - gate), 0.0)

    def attend(delta):
        other = flip_all(me_s, delta)
        for p in range(pairs):
            values = kv[other, pairs + p]
            low = dot(w_sc[delta, p, 0], values)
            high = dot(w_sc[delta, p, 1], values)
            att[p] = att[p] + jnp.where(lane_is_low, low, high)

    att[...] = jnp.zeros_like(att)
    dq[...] = jnp.zeros_like(dq)
    dk[...] = jnp.zeros_like(dk)
    dv[...] = jnp.zeros_like(dv)
    scores_of(0)
    attend(0)
    for delta in range(1, seqs):
        other = flip_all(me_s, delta)
        take(*kv_set, delta)
        take(*q_set, delta)

        @pl.when(other < me_s)
        def _():
            scores_of(delta)
            attend(delta)

    attended = jnp.concatenate([att[p] for p in range(pairs)], axis=1)
    onorm, inverse = layer_norm(attended)
    gate_u = gate_sc[...].astype(F32)
    mixed = (onorm * gate_u).astype(BF16)
    d_mixed = dot(d_out, out_w_ref[...], (1, 1))
    d_gate_u = d_mixed * onorm
    d_onorm = d_mixed * gate_u
    d_att = (
        d_onorm
        - jnp.mean(d_onorm, axis=-1, keepdims=True)
        - onorm * jnp.mean(d_onorm * onorm, axis=-1, keepdims=True)
    ) * inverse
    d_att = d_att.astype(BF16)
    for p in range(pairs):
        gb[me_s, p] = d_att[:, p * LANES : (p + 1) * LANES]
    start_own(*g_set)
    projected_u = proj_sc[:, :width]
    dproj[:, :width] = (d_gate_u * silu_grad(projected_u)).astype(BF16)
    result = dot(mixed, out_w_ref[...]) + out_b_ref[...] + seq_sc[...].astype(F32)
    layer_ref[...] = jnp.where(present, result, 0.0).astype(BF16)
    bias[0] = jnp.zeros_like(bias[0])
    bias[0, 1:2, :model] = jnp.sum(d_out.astype(F32), axis=0, keepdims=True)
    (early, late), stages, total_chunks = plan_of(users, seqs, groups_of(model, width))
    late_base = late[0][0]

    def store_tiles(base, values):
        height = values.shape[0] // ROWS
        for tile in range(values.shape[1] // LANES):
            work[base + tile * height : base + (tile + 1) * height] = values[
                :, tile * LANES : (tile + 1) * LANES
            ].reshape(height, ROWS, LANES)
        return base + values.shape[0] * values.shape[1] // (ROWS * LANES)

    def clear(base, stop):
        if base < stop:
            work[base:stop] = jnp.zeros((stop - base, ROWS, LANES), BF16)

    filled = store_tiles(0, dot(mixed, d_out, (0, 0)).astype(BF16))
    filled = store_tiles(filled, dot(norm_sc[...], dproj[:, :width], (0, 0)).astype(BF16))
    clear(filled, late_base)

    def place_of(axis, bit):
        mine = me_s if axis == "seq" else me_u
        peer = flip(mine, bit)
        device = (me_u, peer) if axis == "seq" else (peer, me_s)
        return (mine // bit) % 2, device

    all_streams = early + late
    starts = [[base] for base, _, _ in all_streams]
    landings = []
    landing_at = 0
    for base, size, _ in all_streams:
        offsets = []
        for stage in range(stages):
            offsets.append(landing_at)
            landing_at += size >> (stage + 1)
        landings.append(offsets)
    early_ids = list(range(len(early)))
    late_ids = list(range(len(early), len(all_streams)))

    def reduce_copy(i, stage):
        base, size, bit_order = all_streams[i]
        side, device = place_of(*bit_order[stage])
        half = size >> (stage + 1)
        start = starts[i][stage]
        return (
            pltpu.make_async_remote_copy(
                src_ref=work.at[pl.ds(start + (1 - side) * half, half)],
                dst_ref=landing.at[pl.ds(landings[i][stage], half)],
                send_sem=rs_send.at[i, stage],
                recv_sem=rs_recv.at[i, stage],
                device_id=device,
                device_id_type=MESH,
            ),
            start + side * half,
            half,
        )

    def gather_copy(i, stage):
        base, size, bit_order = all_streams[i]
        _, device = place_of(*bit_order[stage])
        half = size >> (stage + 1)
        own = full.at[pl.ds(starts[i][stage + 1], half)]
        return pltpu.make_async_remote_copy(
            src_ref=own,
            dst_ref=own,
            send_sem=ag_send.at[i, stage],
            recv_sem=ag_recv.at[i, stage],
            device_id=device,
            device_id_type=MESH,
        )

    def reduce_start(ids):
        for i in ids:
            reduce_copy(i, 0)[0].start()

    def reduce_step(ids, stage):
        for i in ids:
            copy, keep, half = reduce_copy(i, stage)
            copy.wait()
            at = landings[i][stage]
            summed = (
                work[pl.ds(keep, half)].astype(F32) + landing[at : at + half].astype(F32)
            ).astype(BF16)
            starts[i].append(keep)
            if stage + 1 < stages:
                work[pl.ds(keep, half)] = summed
                reduce_copy(i, stage + 1)[0].start()
            else:
                full[pl.ds(keep, half)] = summed
                gather_copy(i, stage).start()

    def gather_step(ids, stage):
        for i in ids:
            gather_copy(i, stage).wait()
            if stage > 0:
                gather_copy(i, stage - 1).start()

    reduce_start(early_ids)

    for delta in range(1, seqs):
        other = flip_all(me_s, delta)

        @pl.when(other > me_s)
        def _():
            scores_of(delta)

    reduce_step(early_ids, 0)

    def backward(delta):
        other = flip_all(me_s, delta)
        q_index = jnp.maximum(other, me_s)
        k_index = jnp.minimum(other, me_s)
        for p in range(pairs):
            grads = gb[q_index, p]
            values = kv[k_index, pairs + p]
            d_scores = []
            for hh in range(2):
                d_weight = dot(half_of(grads, hh), values, (1, 1))
                d_scores.append((d_weight * s_sc[delta, p, hh]).astype(BF16))

            def query_side():
                keys = kv[k_index, p]
                dq[p] = dq[p] + jnp.where(
                    lane_is_low, dot(d_scores[0], keys), dot(d_scores[1], keys)
                )

            def key_side():
                queries = qb[q_index, p]
                dk[p] = dk[p] + jnp.where(
                    lane_is_low,
                    dot(d_scores[0], queries, (0, 0)),
                    dot(d_scores[1], queries, (0, 0)),
                )
                dv[p] = dv[p] + jnp.where(
                    lane_is_low,
                    dot(w_sc[delta, p, 0], grads, (0, 0)),
                    dot(w_sc[delta, p, 1], grads, (0, 0)),
                )

            if delta == 0:
                query_side()
                key_side()
            else:
                pl.when(other < me_s)(query_side)
                pl.when(other > me_s)(key_side)

    backward(0)
    for delta in range(1, seqs):
        other = flip_all(me_s, delta)

        @pl.when(other < me_s)
        def _():
            backward(delta)

    reduce_step(early_ids, 1)
    for delta in range(1, seqs):
        other = flip_all(me_s, delta)
        take(*g_set, delta)

        @pl.when(other > me_s)
        def _():
            backward(delta)

    reduce_step(early_ids, 2)
    early_done = 3
    for part, buf, factor in ((1, dv, 1.0), (2, dq, scale), (3, dk, scale)):
        slope = silu_grad(proj_sc[:, part * width : (part + 1) * width])
        for p in range(pairs):
            low = part * width + p * LANES
            dproj[:, low : low + LANES] = (
                buf[p] * factor * slope[:, p * LANES : (p + 1) * LANES]
            ).astype(BF16)

    d_proj = dproj[...]
    filled = store_tiles(late_base, dot(norm_sc[...], d_proj[:, width:], (0, 0)).astype(BF16))
    clear(filled, total_chunks)
    reduce_start(late_ids)
    bias[0, 0:1, :] = jnp.sum(d_proj.astype(F32), axis=0, keepdims=True)

    def bias_copy(stage):
        _, device = place_of(*all_streams[0][2][stage])
        return pltpu.make_async_remote_copy(
            src_ref=bias.at[stage],
            dst_ref=bias_in.at[stage],
            send_sem=b_send.at[stage],
            recv_sem=b_recv.at[stage],
            device_id=device,
            device_id_type=MESH,
        )

    def bias_step(stage):
        bias_copy(stage).wait()
        bias[stage + 1] = bias[stage] + bias_in[stage]
        if stage + 1 < stages:
            bias_copy(stage + 1).start()

    bias_copy(0).start()
    for turn in range(2 * stages):
        if turn < stages:
            reduce_step(late_ids, turn)
            bias_step(turn)
        else:
            gather_step(late_ids, 2 * stages - 1 - turn)
        ahead = turn + early_done
        if ahead < stages:
            reduce_step(early_ids, ahead)
        elif ahead < 2 * stages:
            gather_step(early_ids, 2 * stages - 1 - ahead)
    bias_ref[...] = bias[stages]
    finish(*kv_set)
    finish(*q_set)
    finish(*g_set)


def unpack(full, bias_ref, layer_in, layer_ref, gpw_ref, gpb_ref, gow_ref, gob_ref, late_base):
    model, width = gow_ref.shape[1], gow_ref.shape[0]
    layer_ref[...] = layer_in[...]
    gpb_ref[...] = bias_ref[0:1, :]
    gob_ref[...] = bias_ref[1:2, :model]

    def tile_of(base, height):
        return full[base : base + height // ROWS].reshape(height, LANES)

    at = 0
    for tile in range(model // LANES):
        gow_ref[:, tile * LANES : (tile + 1) * LANES] = tile_of(at, width)
        at += width // ROWS
    for tile in range(4 * width // LANES):
        if tile == width // LANES:
            at = late_base
        gpw_ref[:, tile * LANES : (tile + 1) * LANES] = tile_of(at, model)
        at += model // ROWS


def on_device(
    users,
    seqs,
    raw_events,
    target_user,
    target_place,
    send_counts,
    lengths,
    cotangent,
    encoder_in,
    encoder_out,
    proj_weight,
    proj_bias,
    out_weight,
    out_bias,
):
    slots = raw_events.shape[1]
    block, model = cotangent.shape[1], cotangent.shape[2]
    width = out_weight.shape[0]
    pairs = width // LANES
    cap_pad = -(-(slots // users) // ROWS) * ROWS
    (early, late), stages, total = plan_of(users, seqs, groups_of(model, width))
    count = len(early) + len(late)
    vmem = pl.BlockSpec(memory_space=pltpu.VMEM)
    anywhere = pl.BlockSpec(memory_space=pl.ANY)
    smem = pl.BlockSpec(memory_space=pltpu.SMEM)
    dma = pltpu.SemaphoreType.DMA
    moves = seqs - 1
    layer, full, bias = pl.pallas_call(
        functools.partial(kernel, users, seqs),
        out_shape=(
            jax.ShapeDtypeStruct((block, model), BF16),
            jax.ShapeDtypeStruct((total, ROWS, LANES), BF16),
            jax.ShapeDtypeStruct((2, 4 * width), F32),
        ),
        in_specs=[anywhere, vmem, vmem, smem, smem] + [anywhere] * 4 + [vmem, anywhere, vmem],
        out_specs=(vmem,) * 3,
        scratch_shapes=[
            pltpu.VMEM((users, cap_pad, model), BF16),
            pltpu.VMEM((users, cap_pad, model), BF16),
            pltpu.VMEM((users, 1, LANES), F32),
            pltpu.VMEM((users, 1, LANES), F32),
            pltpu.VMEM((block, model), BF16),
            pltpu.VMEM((block, model), BF16),
            pltpu.VMEM((block, 4 * width), F32),
            pltpu.VMEM((block, width), BF16),
            pltpu.VMEM((seqs, 2 * pairs, block, LANES), BF16),
            pltpu.VMEM((seqs, pairs, block, LANES), BF16),
            pltpu.VMEM((seqs, pairs, block, LANES), BF16),
            pltpu.VMEM((seqs, pairs, 2, block, block), BF16),
            pltpu.VMEM((seqs, pairs, 2, block, block), F32),
            pltpu.VMEM((pairs, block, LANES), F32),
            pltpu.VMEM((pairs, block, LANES), F32),
            pltpu.VMEM((pairs, block, LANES), F32),
            pltpu.VMEM((pairs, block, LANES), F32),
            pltpu.VMEM((block, 4 * width), BF16),
            pltpu.VMEM((total, ROWS, LANES), BF16),
            pltpu.VMEM((total, ROWS, LANES), BF16),
            pltpu.VMEM((stages + 1, 2, 4 * width), F32),
            pltpu.VMEM((stages, 2, 4 * width), F32),
            dma((users,)),
            dma((users,)),
            dma((users,)),
            dma((users,)),
            dma((moves,)),
            dma((seqs,)),
            dma((moves,)),
            dma((seqs,)),
            dma((moves,)),
            dma((seqs,)),
            dma((count, stages)),
            dma((count, stages)),
            dma((count, stages)),
            dma((count, stages)),
            dma((stages,)),
            dma((stages,)),
            pltpu.VMEM(raw_events.shape[1:], BF16),
            pltpu.VMEM(cotangent.shape[1:], BF16),
            pltpu.VMEM(encoder_in.shape, BF16),
            pltpu.VMEM(encoder_out.shape, BF16),
            pltpu.VMEM(proj_weight.shape, BF16),
            pltpu.VMEM(out_weight.shape, BF16),
            dma((6,)),
        ],
        compiler_params=pltpu.CompilerParams(
            collective_id=0, has_side_effects=True, vmem_limit_bytes=60000 * 1024
        ),
    )(
        raw_events[0],
        target_user,
        target_place,
        send_counts[0],
        lengths,
        cotangent[0],
        encoder_in,
        encoder_out,
        proj_weight,
        proj_bias[None],
        out_weight,
        out_bias[None],
    )
    layer_out, grad_pw, grad_pb, grad_ow, grad_ob = pl.pallas_call(
        functools.partial(unpack, late_base=late[0][0]),
        out_shape=(
            jax.ShapeDtypeStruct((block, model), BF16),
            jax.ShapeDtypeStruct((model, 4 * width), BF16),
            jax.ShapeDtypeStruct((1, 4 * width), F32),
            jax.ShapeDtypeStruct((width, model), BF16),
            jax.ShapeDtypeStruct((1, model), F32),
        ),
        in_specs=[vmem] * 3,
        out_specs=(vmem,) * 5,
    )(full, bias, layer)
    return layer_out[None], grad_pw, grad_pb[0], grad_ow, grad_ob[0]


def solution(mesh):
    placed = (
        P("seq", "users", None),
        P("seq", "users"),
        P("seq", "users"),
        P("seq", "users", None),
        P("users"),
        P("users", "seq", None),
        P(),
        P(),
        P(),
        P(),
        P(),
        P(),
    )
    return jax.shard_map(
        functools.partial(on_device, mesh.shape["users"], mesh.shape["seq"]),
        mesh=mesh,
        in_specs=placed,
        out_specs=(P("users", "seq", None), P(), P(), P(), P()),
        check_vma=False,
    )
```

profile of v0, /device:TPU:0, one launch (start us, length us, event | category | flops | bytes accessed | tf_op | source)
XLA Modules:
  0.0 70.5 jit_solution(4085877292762208998)
XLA Ops:
  1.3 66.3 %shard_map.155 = (bf16[256,512]{1,0:T(8,128)(2,1)}, bf16[320,16,128]{2,1,0:T(8,128)(2,1)}, f32[2,1024]{1,0:T(2,128)}) custom-call(bf16[384,512]{1,0:T(8,128)(2,1)} %bitcast.8, s32[1,384]{1,0:T(1,128)} %user_ref.1, s32[1,384]{1,0:T(1,128)} %place_ref.1, s32[1,8]{1,0:T(1,128)} %bitcast.12, s32[1]{0:T(128)S(6)} %copy.17.length_ref, bf16[256,512]{1,0:T(8,128)(2,1)} %bitcast.9, ...), custom_call_target="tpu_custom_call" | custom-call | tf_op jit(solution)/shard_map/pallas_call | solution.py:685
  67.6 2.8 %shard_map.156 = (bf16[256,512]{1,0:T(8,128)(2,1)}, bf16[512,1024]{1,0:T(8,128)(2,1)}, f32[1,1024]{1,0:T(1,128)}, bf16[256,512]{1,0:T(8,128)(2,1)}, f32[1,512]{1,0:T(1,128)}) custom-call(bf16[320,16,128]{2,1,0:T(8,128)(2,1)} %get-tuple-element.13.full, f32[2,1024]{1,0:T(2,128)} %get-tuple-element.14.bias_ref, bf16[256,512]{1,0:T(8,128)(2,1)} %get-tuple-element.15.layer_in), custom_call_target="tpu_custom_call" | custom-call | tf_op jit(solution)/shard_map/pallas_call | solution.py:758
where the time goes:
time: 70.7 us; the launch traced here: 70.5 us
  Pallas kernels  69.2 us (98%)
  between operations  1.29 us (2%)
    pallas_call x1, Pallas kernels, on_device(): pl.pallas_call(functools.partial(kernel, users, seqs), out_shape=(jax.Sha...  66.3 us
    pallas_call x1, Pallas kernels, on_device(): pl.pallas_call(functools.partial(unpack, late_base=late[0][0]), out_shape...  2.84 us

commit v1 on v0

v1 whole, which is shorter than its diff:
```python
import functools

import jax
import jax.numpy as jnp
from jax import lax
from jax.experimental import pallas as pl
from jax.experimental.pallas import tpu as pltpu
from jax.sharding import PartitionSpec as P

HEAD = 64
EPSILON = 1e-05
LANES = 128
ROWS = 16
F32 = jnp.float32
BF16 = jnp.bfloat16


def sigmoid(values):
    return 0.5 * jnp.tanh(0.5 * values) + 0.5


def silu(values):
    return values * sigmoid(values)


def silu_grad(values):
    gate = sigmoid(values)
    return gate * (1.0 + values * (1.0 - gate))


def layer_norm(values):
    center = values - jnp.mean(values, axis=-1, keepdims=True)
    inverse = lax.rsqrt(jnp.mean(center * center, axis=-1, keepdims=True) + EPSILON)
    return center * inverse, inverse


def dot(a, b, contract=(1, 0)):
    return lax.dot_general(
        a, b, (((contract[0],), (contract[1],)), ((), ())), preferred_element_type=F32
    )


def flip(index, bit):
    return index + bit * (1 - 2 * ((index // bit) % 2))


def flip_all(index, delta):
    bit = 1
    while bit <= delta:
        if delta & bit:
            index = flip(index, bit)
        bit *= 2
    return index


def plan_of(users, seqs, groups):
    near, far = [], []
    bit = 1
    while bit < users:
        near.append(("users", bit))
        bit *= 2
    bit = 2
    while bit < seqs:
        far.append(("seq", bit))
        bit *= 2
    devices = users * seqs // 2
    plans = []
    base = 0
    for chunks, most, across_first in groups:
        each = -(-chunks // devices)
        if across_first:
            turn = (far + near)[:3]
            tail = (far + near)[3:]
        else:
            turn = near[:2]
            tail = near[2:] + far
        streams = []
        for i in range(most):
            share = (each + most - 1 - i) // most
            if share == 0:
                continue
            k = i % len(turn)
            streams.append((base, share * devices, turn[k:] + turn[:k] + tail))
            base += share * devices
        plans.append(streams)
    return plans, len(near) + len(far), base


def groups_of(model, share):
    tile = ROWS * LANES
    return (
        (2 * model * share // tile, 2, False),
        (model * share // tile, 2, False),
        (2 * model * share // tile, 4, True),
    )


def kernel(
    users,
    seqs,
    raw_hbm,
    user_ref,
    place_ref,
    counts_ref,
    length_ref,
    cot_hbm,
    enc_in_hbm,
    enc_out_hbm,
    proj_w_hbm,
    proj_b_ref,
    out_w_hbm,
    out_b_ref,
    layer_ref,
    full,
    bias_ref,
    send_buf,
    rows_sc,
    spot_out,
    spot_in,
    seq_sc,
    norm_sc,
    proj_sc,
    gate_sc,
    v_sc,
    k_sc,
    qb,
    gb,
    w_sc,
    s_sc,
    att,
    dq,
    dk,
    dv,
    d_mix,
    dproj,
    stat_out,
    stat_in,
    mix_own,
    mix_in,
    work,
    landing,
    bias,
    bias_in,
    raw_ref,
    cots,
    enc_in_ref,
    enc_out_ref,
    proj_w_ref,
    out_w_ref,
    a2a_send,
    a2a_recv,
    spot_send,
    spot_recv,
    x_send,
    x_recv,
    xs_send,
    xs_recv,
    n_send,
    n_recv,
    cot_sem,
    stat_sem,
    mix_sem,
    q_send,
    q_recv,
    g_send,
    g_recv,
    rs_send,
    rs_recv,
    ag_send,
    ag_recv,
    core_send,
    core_recv,
    b_send,
    b_recv,
    in_sem,
):
    me_u = lax.axis_index("users")
    me_s = lax.axis_index("seq")
    MESH = pl.DeviceIdType.MESH
    slots, model = raw_ref.shape
    block = layer_ref.shape[0]
    span = 2 * block
    width = out_w_ref.shape[0]
    share = width // 2
    pairs = share // LANES
    cap_pad = send_buf.shape[1]
    halves = seqs // 2
    scale = HEAD ** (-0.5)
    mine = me_s % 2
    half = me_s // 2
    partner = (me_u, flip(me_s, 1))

    def at_half(h):
        return (me_u, h * 2 + mine)

    def remote(source, target, send_sem, recv_sem, device):
        return pltpu.make_async_remote_copy(
            src_ref=source,
            dst_ref=target,
            send_sem=send_sem,
            recv_sem=recv_sem,
            device_id=device,
            device_id_type=MESH,
        )

    barrier = pltpu.get_barrier_semaphore()
    greeted = [(lax.rem(me_u + delta, users), me_s) for delta in range(1, users)]
    greeted += [partner]
    greeted += [at_half(lax.rem(half + delta, halves)) for delta in range(1, halves)]
    for device in greeted:
        pl.semaphore_signal(barrier, inc=1, device_id=device, device_id_type=MESH)

    def own_columns(part):
        return pl.ds(pl.multiple_of(part * width + mine * share, LANES), share)

    parts = (0, 2, 1, 3)
    loads = [
        pltpu.make_async_copy(source, target, in_sem.at[i])
        for i, (source, target) in enumerate(
            [
                (raw_hbm, raw_ref),
                (cot_hbm, cots.at[mine]),
                (out_w_hbm, out_w_ref),
                (enc_in_hbm, enc_in_ref),
                (enc_out_hbm, enc_out_ref),
            ]
            + [
                (
                    proj_w_hbm.at[:, own_columns(part)],
                    proj_w_ref.at[:, i * share : (i + 1) * share],
                )
                for i, part in enumerate(parts)
            ]
        )
    ]
    for load in loads:
        load.start()

    target = user_ref[...]
    lane_row = lax.broadcasted_iota(jnp.int32, (1, slots), 1)
    first = jnp.zeros((1, slots), jnp.int32)
    total = jnp.int32(0)
    for u in range(users):
        first = jnp.where(target == u, total, first)
        total = total + counts_ref[0, u]
    flat = jnp.where(lane_row < total, target * cap_pad + lane_row - first, -1)
    hot = lax.broadcasted_iota(jnp.int32, (users * cap_pad, slots), 0) == flat
    local_place = (place_ref[...] - me_s * block + 1).astype(F32)
    spots = jnp.sum(jnp.where(hot, local_place, 0.0), axis=1, keepdims=True) - 1.0
    diagonal = lax.broadcasted_iota(
        jnp.int32, (users, cap_pad, LANES), 1
    ) == lax.broadcasted_iota(jnp.int32, (users, cap_pad, LANES), 2)
    spot_out[...] = jnp.sum(
        jnp.where(diagonal, spots.reshape(users, cap_pad, 1), 0.0), axis=1, keepdims=True
    )
    loads[0].wait()
    bucket = dot(hot.astype(F32).astype(BF16), raw_ref[...]).astype(BF16)
    send_buf[...] = bucket.reshape(users, cap_pad, model)

    pl.semaphore_wait(barrier, len(greeted))

    order = list(range(users - 1, 0, -1))

    def spot_copy(d):
        peer = flip_all(me_u, d)
        return remote(
            spot_out.at[peer], spot_in.at[half, me_u], spot_send.at[d], spot_recv.at[d], (peer, me_s)
        )

    def row_copy(d):
        peer = flip_all(me_u, d)
        return remote(
            send_buf.at[peer], rows_sc.at[half, me_u], a2a_send.at[d], a2a_recv.at[d], (peer, me_s)
        )

    def relay(h, d, delta):
        source = flip_all(me_u, d)
        held = send_buf.at[source] if d == 0 else rows_sc.at[h, source]
        return remote(
            held,
            rows_sc.at[h, source],
            x_send.at[delta - 1, d],
            x_recv.at[delta - 1, d],
            at_half(h + delta),
        )

    def relay_spots(h, delta):
        return remote(
            spot_in.at[h],
            spot_in.at[h],
            xs_send.at[delta - 1],
            xs_recv.at[delta - 1],
            at_half(h + delta),
        )

    def above(delta):
        return half + delta < halves

    def below(delta):
        return half >= delta

    for d in order:
        spot_copy(d).start()
    for d in order:
        row_copy(d).start()
    for delta in range(1, halves):

        @pl.when(above(delta))
        def _():
            relay(half, 0, delta).start()

    loads[1].wait()
    cot_copy = remote(cots.at[mine], cots.at[mine], cot_sem.at[0], cot_sem.at[1], partner)
    cot_copy.start()
    rows_sc[half, me_u] = send_buf[me_u]
    spot_in[half, me_u] = spot_out[me_u]

    length = length_ref[0]
    rows = lax.broadcasted_iota(jnp.int32, (block, 1), 0)

    def block_rows(index):
        return pl.ds(pl.multiple_of(index * block, block), block)

    own_rows, other_rows = block_rows(mine), block_rows(1 - mine)

    def present_at(index):
        return (half * 2 + index) * block + rows < length

    out_rows = pl.ds(pl.multiple_of(mine * share, LANES), share)
    out_rows_other = pl.ds(pl.multiple_of((1 - mine) * share, LANES), share)
    loads[2].wait()

    def mask_cot(index):
        d_out = jnp.where(
            present_at(index), cots[index], jnp.zeros((block, model), BF16)
        )
        d_mix[block_rows(index), :] = dot(d_out, out_w_ref[out_rows, :], (1, 1))

    mask_cot(mine)
    for load in loads[3:]:
        load.wait()
    bias_row = jnp.concatenate([proj_b_ref[:, own_columns(part)] for part in parts], axis=1)
    att[...] = jnp.zeros_like(att)
    dq[...] = jnp.zeros_like(dq)
    dk[...] = jnp.zeros_like(dk)
    dv[...] = jnp.zeros_like(dv)
    cot_copy.wait_recv()
    mask_cot(1 - mine)

    for d in order:
        spot_copy(d).wait_recv()
    for delta in range(1, halves):

        @pl.when(above(delta))
        def _():
            relay_spots(half, delta).start()

    for d in order:
        row_copy(d).wait_recv()
        for delta in range(1, halves):

            @pl.when(above(delta))
            def _():
                relay(half, d, delta).start()

    def ingest(h):
        arrived = rows_sc[h].reshape(users * cap_pad, model)
        where_to = jnp.sum(jnp.where(diagonal, spot_in[h], 0.0), axis=2, keepdims=True)
        where_to = where_to.reshape(users * cap_pad, 1).astype(jnp.int32)
        placed = (
            lax.broadcasted_iota(jnp.int32, (users * cap_pad, block), 1) == where_to
        ).astype(F32).astype(BF16)
        events = dot(placed, arrived, (0, 0)).astype(BF16)
        hidden = silu(dot(events, enc_in_ref[...])).astype(BF16)
        sequence = dot(hidden, enc_out_ref[...]).astype(BF16)
        norm_sc[h, mine] = layer_norm(sequence.astype(F32))[0].astype(BF16)
        return sequence

    def norm_copy(h):
        own = norm_sc.at[h, mine]
        return remote(own, own, n_send.at[h], n_recv.at[h], partner)

    seq_sc[...] = ingest(half)
    norm_copy(half).start()

    def project(index):
        at = block_rows(index)
        projected = dot(norm_sc[half, index], proj_w_ref[...]) + bias_row
        proj_sc[at, :] = projected
        gates = silu(projected).astype(BF16)
        gate_sc[at, :] = gates[:, :share]
        qb[half, at, :] = gates[:, share : 2 * share]
        v_sc[half, at, :] = gates[:, 2 * share : 3 * share]
        k_sc[half, at, :] = gates[:, 3 * share :]

    def project_low(h, index):
        at = block_rows(index)
        gates = silu(
            dot(norm_sc[h, index], proj_w_ref[:, 2 * share :]) + bias_row[:, 2 * share :]
        ).astype(BF16)
        v_sc[h, at, :] = gates[:, :share]
        k_sc[h, at, :] = gates[:, share:]

    project(mine)

    for delta in range(1, halves):

        @pl.when(below(delta))
        def _():
            h = half - delta
            relay_spots(h, delta).wait_recv()
            for d in [0] + order:
                relay(h, d, delta).wait_recv()
            ingest(h)
            norm_copy(h).start()
            project_low(h, mine)

    norm_copy(half).wait_recv()
    project(1 - mine)

    def q_copy(delta):
        return remote(
            qb.at[half], qb.at[half], q_send.at[delta - 1], q_recv.at[delta - 1], at_half(half - delta)
        )

    for delta in range(1, halves):

        @pl.when(below(delta))
        def _():
            q_copy(delta).start()

    def half_of(values, hh):
        zero = jnp.zeros_like(values)
        low = lax.broadcasted_iota(jnp.int32, values.shape, 1) < HEAD
        return jnp.where(low, values, zero) if hh == 0 else jnp.where(low, zero, values)

    def lanes(p):
        return slice(p * LANES, (p + 1) * LANES)

    def merge(low, high):
        keep = lax.broadcasted_iota(jnp.int32, low.shape, 1) < HEAD
        return jnp.where(keep, low, high)

    def scores_of(slot, q_half, k_half, qi, keys_to):
        qr = slice(qi * block, (qi + 1) * block)
        kr = slice(0, keys_to * block)
        bound = jnp.minimum((q_half * 2 + qi) * block + rows, length - 1) - k_half * span
        allowed = lax.broadcasted_iota(jnp.int32, (block, keys_to * block), 1) <= bound
        for p in range(pairs):
            queries = qb[q_half, qr, lanes(p)]
            keys = k_sc[k_half, kr, lanes(p)]
            for hh in range(2):
                score = dot(half_of(queries, hh), keys, (1, 1)) * scale
                gate = sigmoid(score)
                plain = score * gate
                w_sc[slot, 2 * p + hh, qr, kr] = jnp.where(allowed, plain, 0.0).astype(BF16)
                s_sc[slot, 2 * p + hh, qr, kr] = jnp.where(
                    allowed, gate + plain * (1.0 - gate), 0.0
                )

    def attend(slot, k_half, qi, keys_to):
        qr = slice(qi * block, (qi + 1) * block)
        kr = slice(0, keys_to * block)
        for p in range(pairs):
            values = v_sc[k_half, kr, lanes(p)]
            att[qr, lanes(p)] = att[qr, lanes(p)] + merge(
                dot(w_sc[slot, 2 * p, qr, kr], values), dot(w_sc[slot, 2 * p + 1, qr, kr], values)
            )

    for qi in range(2):
        scores_of(half, half, half, qi, qi + 1)
        attend(half, half, qi, qi + 1)

    for delta in range(1, halves):

        @pl.when(below(delta))
        def _():
            h = half - delta
            norm_copy(h).wait_recv()
            project_low(h, 1 - mine)
            for qi in range(2):
                scores_of(h, half, h, qi, 2)
                attend(h, h, qi, 2)

    attended = att[...]
    gate_u = gate_sc[...].astype(F32)
    d_mixed = d_mix[...]
    d_onorm = d_mixed * gate_u
    own_mean = jnp.mean(attended, axis=-1, keepdims=True)
    center = attended - own_mean
    facts = (
        own_mean,
        jnp.sum(center * center, axis=-1, keepdims=True),
        jnp.sum(d_onorm, axis=-1, keepdims=True),
        jnp.sum(d_onorm * center, axis=-1, keepdims=True),
    )
    tall = span // LANES
    square = lax.broadcasted_iota(jnp.int32, (tall, LANES, LANES), 1) == lax.broadcasted_iota(
        jnp.int32, (tall, LANES, LANES), 2
    )
    for i, fact in enumerate(facts):
        stat_out[i] = jnp.sum(
            jnp.where(square, fact.reshape(tall, LANES, 1), 0.0), axis=1, keepdims=True
        )
    stat_copy = remote(stat_out, stat_in, stat_sem.at[0], stat_sem.at[1], partner)
    stat_copy.start()

    stat_copy.wait_recv()
    theirs = [
        jnp.sum(jnp.where(square, stat_in[i], 0.0), axis=2, keepdims=True).reshape(span, 1)
        for i in range(len(facts))
    ]
    mean = 0.5 * (own_mean + theirs[0])
    gap = own_mean - theirs[0]
    variance = (facts[1] + theirs[1] + gap * gap * (0.5 * share)) / width
    inverse = lax.rsqrt(variance + EPSILON)
    mean_d = (facts[2] + theirs[2]) / width
    mean_do = (
        (facts[3] + theirs[3] + (own_mean - mean) * facts[2] + (theirs[0] - mean) * theirs[2])
        * inverse
        / width
    )
    onorm = (attended - mean) * inverse
    d_att = ((d_onorm - mean_d - onorm * mean_do) * inverse).astype(BF16)
    gb[half] = d_att

    def g_copy(delta, qi):
        piece = gb.at[half, qi * block : (qi + 1) * block]
        return remote(
            piece, piece, g_send.at[delta - 1, qi], g_recv.at[delta - 1, qi], at_half(half - delta)
        )

    for delta in range(1, halves):

        @pl.when(below(delta))
        def _():
            for qi in range(2):
                g_copy(delta, qi).start()

    mixed = (onorm * gate_u).astype(BF16)
    mix_own[...] = mixed
    mix_copy = remote(mix_own.at[other_rows], mix_in, mix_sem.at[0], mix_sem.at[1], partner)
    mix_copy.start()
    dproj[:, :share] = (d_mixed * onorm * silu_grad(proj_sc[:, :share])).astype(BF16)
    positions = lax.broadcasted_iota(jnp.int32, (span, 1), 0)
    present = half * span + positions < length
    d_out = jnp.where(present, cots[...].reshape(span, model), jnp.zeros((span, model), BF16))
    normed = norm_sc[half].reshape(span, model)
    column = jnp.sum(d_out.astype(F32), axis=0, keepdims=True)
    bias[0] = jnp.zeros_like(bias[0])
    bias[0, 1:2, : model // 2] = jnp.where(
        mine == 0, column[:, : model // 2], column[:, model // 2 :]
    )
    (early, middle, late), stages, total_chunks = plan_of(users, seqs, groups_of(model, share))
    middle_base, late_base = middle[0][0], late[0][0]

    def store_tiles(base, values):
        height = values.shape[0] // ROWS
        for tile in range(values.shape[1] // LANES):
            work[base + tile * height : base + (tile + 1) * height] = values[
                :, tile * LANES : (tile + 1) * LANES
            ].reshape(height, ROWS, LANES)
        return base + values.shape[0] * values.shape[1] // (ROWS * LANES)

    def clear(base, stop):
        if base < stop:
            work[base:stop] = jnp.zeros((stop - base, ROWS, LANES), BF16)

    filled = store_tiles(0, dot(mixed, d_out, (0, 0)).astype(BF16))
    filled = store_tiles(filled, dot(normed, dproj[:, :share], (0, 0)).astype(BF16))
    clear(filled, middle_base)

    def place_of(axis, bit):
        own = me_s if axis == "seq" else me_u
        peer = flip(own, bit)
        device = (me_u, peer) if axis == "seq" else (peer, me_s)
        return (own // bit) % 2, device

    all_streams = early + middle + late
    starts = [[base] for base, _, _ in all_streams]
    landings = []
    landing_at = 0
    for base, size, _ in all_streams:
        offsets = []
        for stage in range(stages):
            offsets.append(landing_at)
            landing_at += size >> (stage + 1)
        landings.append(offsets)
    early_ids = list(range(len(early)))
    middle_ids = list(range(len(early), len(early) + len(middle)))
    late_ids = list(range(len(early) + len(middle), len(all_streams)))

    def reduce_copy(i, stage):
        base, size, bit_order = all_streams[i]
        side, device = place_of(*bit_order[stage])
        part = size >> (stage + 1)
        start = starts[i][stage]
        return (
            remote(
                work.at[pl.ds(start + (1 - side) * part, part)],
                landing.at[pl.ds(landings[i][stage], part)],
                rs_send.at[i, stage],
                rs_recv.at[i, stage],
                device,
            ),
            start + side * part,
            part,
        )

    def gather_copy(i, stage):
        base, size, bit_order = all_streams[i]
        _, device = place_of(*bit_order[stage])
        own = full.at[mine, pl.ds(starts[i][stage + 1], size >> (stage + 1))]
        return remote(own, own, ag_send.at[i, stage], ag_recv.at[i, stage], device)

    def core_copy(i, second):
        base, size, bit_order = all_streams[i]
        side, _ = place_of(*bit_order[0])
        part = size >> 1
        start = base + (1 - side) * part if second else base + side * part
        own = full.at[mine, pl.ds(start, part)]
        return remote(own, own, core_send.at[i, second], core_recv.at[i, second], partner)

    def reduce_start(ids):
        for i in ids:
            reduce_copy(i, 0)[0].start()

    def reduce_step(ids, stage):
        for i in ids:
            copy, keep, part = reduce_copy(i, stage)
            copy.wait()
            at = landings[i][stage]
            summed = (
                work[pl.ds(keep, part)].astype(F32) + landing[at : at + part].astype(F32)
            ).astype(BF16)
            starts[i].append(keep)
            if stage + 1 < stages:
                work[pl.ds(keep, part)] = summed
                reduce_copy(i, stage + 1)[0].start()
            else:
                full[mine, pl.ds(keep, part)] = summed
                gather_copy(i, stage).start()
                if stage == 0:
                    core_copy(i, 0).start()

    def gather_step(ids, stage):
        for i in ids:
            gather_copy(i, stage).wait()
            if stage > 0:
                gather_copy(i, stage - 1).start()
                if stage == 1:
                    core_copy(i, 0).start()
            else:
                core_copy(i, 1).start()

    def core_finish(ids):
        for i in ids:
            core_copy(i, 0).wait()
            core_copy(i, 1).wait()

    def advance(ids, turn):
        if turn < stages:
            reduce_step(ids, turn)
        elif turn < 2 * stages:
            gather_step(ids, 2 * stages - 1 - turn)
        elif turn == 2 * stages:
            core_finish(ids)

    reduce_start(early_ids)

    for delta in range(1, halves):

        @pl.when(above(delta))
        def _():
            h = half + delta
            remote(
                qb.at[h], qb.at[h], q_send.at[delta - 1], q_recv.at[delta - 1], at_half(half)
            ).wait_recv()
            for qi in range(2):
                scores_of(h, h, half, qi, 2)

    def backward(slot, q_half, k_half, qi, keys_to, query_side, key_side):
        qr = slice(qi * block, (qi + 1) * block)
        kr = slice(0, keys_to * block)
        for p in range(pairs):
            at = lanes(p)
            grads = gb[q_half, qr, at]
            values = v_sc[k_half, kr, at]
            d_scores = []
            for hh in range(2):
                d_weight = dot(half_of(grads, hh), values, (1, 1))
                d_scores.append((d_weight * s_sc[slot, 2 * p + hh, qr, kr]).astype(BF16))
            if query_side:
                keys = k_sc[k_half, kr, at]
                dq[qr, at] = dq[qr, at] + merge(dot(d_scores[0], keys), dot(d_scores[1], keys))
            if key_side:
                queries = qb[q_half, qr, at]
                dk[kr, at] = dk[kr, at] + merge(
                    dot(d_scores[0], queries, (0, 0)), dot(d_scores[1], queries, (0, 0))
                )
                dv[kr, at] = dv[kr, at] + merge(
                    dot(w_sc[slot, 2 * p, qr, kr], grads, (0, 0)),
                    dot(w_sc[slot, 2 * p + 1, qr, kr], grads, (0, 0)),
                )

    for qi in range(2):
        backward(half, half, half, qi, qi + 1, True, True)

    for delta in range(1, halves):

        @pl.when(below(delta))
        def _():
            h = half - delta
            for qi in range(2):
                backward(h, half, h, qi, 2, True, False)

    def finish_part(index, buf, factor):
        at = slice(index * share, (index + 1) * share)
        dproj[:, at] = (buf[...] * factor * silu_grad(proj_sc[:, at])).astype(BF16)

    finish_part(1, dq, scale)
    filled = store_tiles(
        middle_base, dot(normed, dproj[:, share : 2 * share], (0, 0)).astype(BF16)
    )
    clear(filled, late_base)
    reduce_start(middle_ids)

    advance(early_ids, 0)
    advance(early_ids, 1)

    for delta in range(1, halves):

        @pl.when(above(delta))
        def _():
            h = half + delta
            for qi in range(2):
                piece = gb.at[h, qi * block : (qi + 1) * block]
                remote(
                    piece, piece, g_send.at[delta - 1, qi], g_recv.at[delta - 1, qi], at_half(half)
                ).wait_recv()
                backward(h, h, half, qi, 2, False, True)

    finish_part(2, dv, 1.0)
    finish_part(3, dk, scale)
    filled = store_tiles(late_base, dot(normed, dproj[:, 2 * share :], (0, 0)).astype(BF16))
    clear(filled, total_chunks)
    reduce_start(late_ids)
    bias[0, 0:1, :] = jnp.sum(dproj[...].astype(F32), axis=0, keepdims=True)

    def bias_copy(stage):
        _, device = place_of(*all_streams[late_ids[0]][2][stage])
        return remote(
            bias.at[stage], bias_in.at[stage], b_send.at[stage], b_recv.at[stage], device
        )

    def bias_step(stage):
        bias_copy(stage).wait()
        bias[stage + 1] = bias[stage] + bias_in[stage]
        if stage + 1 < stages:
            bias_copy(stage + 1).start()

    bias_copy(0).start()

    mix_copy.wait_recv()
    result = (
        dot(mix_own[own_rows, :], out_w_ref[out_rows, :])
        + dot(mix_in[...], out_w_ref[out_rows_other, :])
        + out_b_ref[...]
        + seq_sc[...].astype(F32)
    )
    layer_ref[...] = jnp.where(present_at(mine), result, 0.0).astype(BF16)

    for turn in range(2 * stages + 1):
        advance(late_ids, turn)
        if turn < stages:
            bias_step(turn)
        if turn == stages:
            bias_ref[mine] = bias[stages]
            bias_own = bias_ref.at[mine]
            bias_final = remote(bias_own, bias_own, b_send.at[stages], b_recv.at[stages], partner)
            bias_final.start()
        advance(middle_ids, turn)
        advance(early_ids, turn + 2)

    bias_final.wait()
    for d in order:
        spot_copy(d).wait_send()
        row_copy(d).wait_send()
    cot_copy.wait_send()
    stat_copy.wait_send()
    mix_copy.wait_send()
    norm_copy(half).wait_send()
    for delta in range(1, halves):

        @pl.when(above(delta))
        def _():
            relay_spots(half, delta).wait_send()
            for d in [0] + order:
                relay(half, d, delta).wait_send()

        @pl.when(below(delta))
        def _():
            norm_copy(half - delta).wait_send()
            q_copy(delta).wait_send()
            for qi in range(2):
                g_copy(delta, qi).wait_send()


def unpack(full, bias_ref, layer_in, layer_ref, gpw_ref, gpb_ref, gow_ref, gob_ref, bases):
    model, width = gow_ref.shape[1], gow_ref.shape[0]
    share = width // 2
    layer_ref[...] = layer_in[...]

    for plane in range(2):
        for i, part in enumerate((0, 2, 1, 3)):
            low = part * width + plane * share
            gpb_ref[:, low : low + share] = bias_ref[plane, 0:1, i * share : (i + 1) * share]
        low = plane * (model // 2)
        gob_ref[:, low : low + model // 2] = bias_ref[plane, 1:2, : model // 2]

        def tile_of(base, height):
            return full[plane, base : base + height // ROWS].reshape(height, LANES)

        at = 0
        rows = slice(plane * share, (plane + 1) * share)
        for tile in range(model // LANES):
            gow_ref[rows, tile * LANES : (tile + 1) * LANES] = tile_of(at, share)
            at += share // ROWS
        size = model // ROWS
        per = share // LANES
        spots = (
            (0, at),
            (2, bases[1]),
            (1, bases[2]),
            (3, bases[2] + per * size),
        )
        for part, at in spots:
            for tile in range(per):
                low = part * width + plane * share + tile * LANES
                gpw_ref[:, low : low + LANES] = tile_of(at + tile * size, model)


def on_device(
    users,
    seqs,
    raw_events,
    target_user,
    target_place,
    send_counts,
    lengths,
    cotangent,
    encoder_in,
    encoder_out,
    proj_weight,
    proj_bias,
    out_weight,
    out_bias,
):
    slots = raw_events.shape[1]
    block, model = cotangent.shape[1], cotangent.shape[2]
    width = out_weight.shape[0]
    share = width // 2
    span = 2 * block
    halves = seqs // 2
    heads = share // HEAD
    others = max(halves - 1, 1)
    cap_pad = -(-(slots // users) // ROWS) * ROWS
    plans, stages, total = plan_of(users, seqs, groups_of(model, share))
    count = sum(len(plan) for plan in plans)
    vmem = pl.BlockSpec(memory_space=pltpu.VMEM)
    anywhere = pl.BlockSpec(memory_space=pl.ANY)
    smem = pl.BlockSpec(memory_space=pltpu.SMEM)
    dma = pltpu.SemaphoreType.DMA
    layer, full, bias = pl.pallas_call(
        functools.partial(kernel, users, seqs),
        out_shape=(
            jax.ShapeDtypeStruct((block, model), BF16),
            jax.ShapeDtypeStruct((2, total, ROWS, LANES), BF16),
            jax.ShapeDtypeStruct((2, 2, 4 * share), F32),
        ),
        in_specs=[anywhere, vmem, vmem, smem, smem] + [anywhere] * 4 + [vmem, anywhere, vmem],
        out_specs=(vmem,) * 3,
        scratch_shapes=[
            pltpu.VMEM((users, cap_pad, model), BF16),
            pltpu.VMEM((halves, users, cap_pad, model), BF16),
            pltpu.VMEM((users, 1, LANES), F32),
            pltpu.VMEM((halves, users, 1, LANES), F32),
            pltpu.VMEM((block, model), BF16),
            pltpu.VMEM((halves, 2, block, model), BF16),
            pltpu.VMEM((span, 4 * share), F32),
            pltpu.VMEM((span, share), BF16),
            pltpu.VMEM((halves, span, share), BF16),
            pltpu.VMEM((halves, span, share), BF16),
            pltpu.VMEM((halves, span, share), BF16),
            pltpu.VMEM((halves, span, share), BF16),
            pltpu.VMEM((halves, heads, span, span), BF16),
            pltpu.VMEM((halves, heads, span, span), F32),
            pltpu.VMEM((span, share), F32),
            pltpu.VMEM((span, share), F32),
            pltpu.VMEM((span, share), F32),
            pltpu.VMEM((span, share), F32),
            pltpu.VMEM((span, share), F32),
            pltpu.VMEM((span, 4 * share), BF16),
            pltpu.VMEM((4, span // LANES, 1, LANES), F32),
            pltpu.VMEM((4, span // LANES, 1, LANES), F32),
            pltpu.VMEM((span, share), BF16),
            pltpu.VMEM((block, share), BF16),
            pltpu.VMEM((total, ROWS, LANES), BF16),
            pltpu.VMEM((total, ROWS, LANES), BF16),
            pltpu.VMEM((stages + 1, 2, 4 * share), F32),
            pltpu.VMEM((stages, 2, 4 * share), F32),
            pltpu.VMEM(raw_events.shape[1:], BF16),
            pltpu.VMEM((2, block, model), BF16),
            pltpu.VMEM(encoder_in.shape, BF16),
            pltpu.VMEM(encoder_out.shape, BF16),
            pltpu.VMEM((model, 4 * share), BF16),
            pltpu.VMEM(out_weight.shape, BF16),
            dma((users,)),
            dma((users,)),
            dma((users,)),
            dma((users,)),
            dma((others, users)),
            dma((others, users)),
            dma((others,)),
            dma((others,)),
            dma((halves,)),
            dma((halves,)),
            dma((2,)),
            dma((2,)),
            dma((2,)),
            dma((others,)),
            dma((others,)),
            dma((others, 2)),
            dma((others, 2)),
            dma((count, stages)),
            dma((count, stages)),
            dma((count, stages)),
            dma((count, stages)),
            dma((count, 2)),
            dma((count, 2)),
            dma((stages + 1,)),
            dma((stages + 1,)),
            dma((9,)),
        ],
        compiler_params=pltpu.CompilerParams(
            collective_id=0, has_side_effects=True, vmem_limit_bytes=60000 * 1024
        ),
    )(
        raw_events[0],
        target_user,
        target_place,
        send_counts[0],
        lengths,
        cotangent[0],
        encoder_in,
        encoder_out,
        proj_weight,
        proj_bias[None],
        out_weight,
        out_bias[None],
    )
    layer_out, grad_pw, grad_pb, grad_ow, grad_ob = pl.pallas_call(
        functools.partial(unpack, bases=[plan[0][0] for plan in plans]),
        out_shape=(
            jax.ShapeDtypeStruct((block, model), BF16),
            jax.ShapeDtypeStruct((model, 4 * width), BF16),
            jax.ShapeDtypeStruct((1, 4 * width), F32),
            jax.ShapeDtypeStruct((width, model), BF16),
            jax.ShapeDtypeStruct((1, model), F32),
        ),
        in_specs=[vmem] * 3,
        out_specs=(vmem,) * 5,
    )(full, bias, layer)
    return layer_out[None], grad_pw, grad_pb[0], grad_ow, grad_ob[0]


def solution(mesh):
    placed = (
        P("seq", "users", None),
        P("seq", "users"),
        P("seq", "users"),
        P("seq", "users", None),
        P("users"),
        P("users", "seq", None),
        P(),
        P(),
        P(),
        P(),
        P(),
        P(),
    )
    return jax.shard_map(
        functools.partial(on_device, mesh.shape["users"], mesh.shape["seq"]),
        mesh=mesh,
        in_specs=placed,
        out_specs=(P("users", "seq", None), P(), P(), P(), P()),
        check_vma=False,
    )
```

time: 70.7 us -> 68.7 us (0.972)
  Pallas kernels: 69.2 us -> 67.3 us
    pallas_call x1, Pallas kernels: 66.3 us -> 64.4 us  [on_device(): pl.pallas_call(functools.partial(kernel, users, seqs), out_shape=(jax.Sha...]
where the time goes in v1:
time: 68.7 us; the launch traced here: 68.5 us
  Pallas kernels  67.3 us (98%)
  between operations  1.29 us (2%)
    pallas_call x1, Pallas kernels, on_device(): pl.pallas_call(functools.partial(kernel, users, seqs), out_shape=(jax.Sha...  64.4 us
    pallas_call x1, Pallas kernels, on_device(): pl.pallas_call(functools.partial(unpack, bases=[plan[0][0] for plan in pl...  2.84 us

profile of v1, /device:TPU:0, one launch (start us, length us, event | category | flops | bytes accessed | tf_op | source)
XLA Modules:
  0.0 68.5 jit_solution(10794399258384331688)
XLA Ops:
  1.3 64.4 %shard_map.155 = (bf16[256,512]{1,0:T(8,128)(2,1)}, bf16[2,160,16,128]{3,2,1,0:T(8,128)(2,1)}, f32[2,2,512]{2,1,0:T(2,128)}) custom-call(bf16[384,512]{1,0:T(8,128)(2,1)} %bitcast.8, s32[1,384]{1,0:T(1,128)} %user_ref.1, s32[1,384]{1,0:T(1,128)} %place_ref.1, s32[1,8]{1,0:T(1,128)} %bitcast.12, s32[1]{0:T(128)S(6)} %copy.17.length_ref, ...), custom_call_target="tpu_custom_call" | custom-call | tf_op jit(solution)/shard_map/pallas_call | solution.py:874
  65.7 2.8 %shard_map.156 = (bf16[256,512]{1,0:T(8,128)(2,1)}, bf16[512,1024]{1,0:T(8,128)(2,1)}, f32[1,1024]{1,0:T(1,128)}, bf16[256,512]{1,0:T(8,128)(2,1)}, f32[1,512]{1,0:T(1,128)}) custom-call(bf16[2,160,16,128]{3,2,1,0:T(8,128)(2,1)} %get-tuple-element.13.full, f32[2,2,512]{2,1,0:T(2,128)} %get-tuple-element.14.bias_ref, bf16[256,512]{1,0:T(8,128)(2,1)} %get-tuple-element.15.layer_in), custom_call_target="tpu_custom_call" | custom-call | tf_op jit(solution)/shard_map/pallas_call | solution.py:962

commit v2 on v1

--- a/solution.py
+++ b/solution.py
@@ -11,6 +11,7 @@
 EPSILON = 1e-05
 LANES = 128
 ROWS = 16
+RESIDENT = 320
 F32 = jnp.float32
 BF16 = jnp.bfloat16
 
@@ -102,7 +103,7 @@
     user_ref,
     place_ref,
     counts_ref,
-    length_ref,
+    length_hbm,
     cot_hbm,
     enc_in_hbm,
     enc_out_hbm,
@@ -173,6 +174,8 @@
     b_send,
     b_recv,
     in_sem,
+    length_sm,
+    length_sem,
 ):
     me_u = lax.axis_index("users")
     me_s = lax.axis_index("seq")
@@ -213,6 +216,8 @@
     def own_columns(part):
         return pl.ds(pl.multiple_of(part * width + mine * share, LANES), share)
 
+    length_load = pltpu.make_async_copy(length_hbm, length_sm, length_sem)
+    length_load.start()
     parts = (0, 2, 1, 3)
     loads = [
         pltpu.make_async_copy(source, target, in_sem.at[i])
@@ -259,7 +264,7 @@
 
     pl.semaphore_wait(barrier, len(greeted))
 
-    order = list(range(users - 1, 0, -1))
+    order = list(range(1, users))
 
     def spot_copy(d):
         peer = flip_all(me_u, d)
@@ -315,7 +320,8 @@
     rows_sc[half, me_u] = send_buf[me_u]
     spot_in[half, me_u] = spot_out[me_u]
 
-    length = length_ref[0]
+    length_load.wait()
+    length = length_sm[0]
     rows = lax.broadcasted_iota(jnp.int32, (block, 1), 0)
 
     def block_rows(index):
@@ -348,20 +354,20 @@
     mask_cot(1 - mine)
 
     for d in order:
+        row_copy(d).wait_recv()
+        for delta in range(1, halves):
+
+            @pl.when(above(delta))
+            def _():
+                relay(half, d, delta).start()
+
+    for d in order:
         spot_copy(d).wait_recv()
     for delta in range(1, halves):
 
         @pl.when(above(delta))
         def _():
             relay_spots(half, delta).start()
-
-    for d in order:
-        row_copy(d).wait_recv()
-        for delta in range(1, halves):
-
-            @pl.when(above(delta))
-            def _():
-                relay(half, d, delta).start()
 
     def ingest(h):
         arrived = rows_sc[h].reshape(users * cap_pad, model)
@@ -401,34 +407,6 @@
         v_sc[h, at, :] = gates[:, :share]
         k_sc[h, at, :] = gates[:, share:]
 
-    project(mine)
-
-    for delta in range(1, halves):
-
-        @pl.when(below(delta))
-        def _():
-            h = half - delta
-            relay_spots(h, delta).wait_recv()
-            for d in [0] + order:
-                relay(h, d, delta).wait_recv()
-            ingest(h)
-            norm_copy(h).start()
-            project_low(h, mine)
-
-    norm_copy(half).wait_recv()
-    project(1 - mine)
-
-    def q_copy(delta):
-        return remote(
-            qb.at[half], qb.at[half], q_send.at[delta - 1], q_recv.at[delta - 1], at_half(half - delta)
-        )
-
-    for delta in range(1, halves):
-
-        @pl.when(below(delta))
-        def _():
-            q_copy(delta).start()
-
     def half_of(values, hh):
         zero = jnp.zeros_like(values)
         low = lax.broadcasted_iota(jnp.int32, values.shape, 1) < HEAD
@@ -441,11 +419,11 @@
         keep = lax.broadcasted_iota(jnp.int32, low.shape, 1) < HEAD
         return jnp.where(keep, low, high)
 
-    def scores_of(slot, q_half, k_half, qi, keys_to):
-        qr = slice(qi * block, (qi + 1) * block)
-        kr = slice(0, keys_to * block)
-        bound = jnp.minimum((q_half * 2 + qi) * block + rows, length - 1) - k_half * span
-        allowed = lax.broadcasted_iota(jnp.int32, (block, keys_to * block), 1) <= bound
+    def scores_of(slot, q_half, qi, k_half, ki):
+        qr, kr = block_rows(qi), block_rows(ki)
+        bound = jnp.minimum((q_half * 2 + qi) * block + rows, length - 1)
+        bound = bound - (k_half * 2 + ki) * block
+        allowed = lax.broadcasted_iota(jnp.int32, (block, block), 1) <= bound
         for p in range(pairs):
             queries = qb[q_half, qr, lanes(p)]
             keys = k_sc[k_half, kr, lanes(p)]
@@ -458,29 +436,62 @@
                     allowed, gate + plain * (1.0 - gate), 0.0
                 )
 
-    def attend(slot, k_half, qi, keys_to):
-        qr = slice(qi * block, (qi + 1) * block)
-        kr = slice(0, keys_to * block)
+    def attend(slot, qi, k_half, ki):
+        qr, kr = block_rows(qi), block_rows(ki)
         for p in range(pairs):
             values = v_sc[k_half, kr, lanes(p)]
             att[qr, lanes(p)] = att[qr, lanes(p)] + merge(
                 dot(w_sc[slot, 2 * p, qr, kr], values), dot(w_sc[slot, 2 * p + 1, qr, kr], values)
             )
 
-    for qi in range(2):
-        scores_of(half, half, half, qi, qi + 1)
-        attend(half, half, qi, qi + 1)
+    project(mine)
+
+    def own_block(qi, ki):
+        scores_of(half, half, qi, half, ki)
+        attend(half, qi, half, ki)
+
+    own_block(mine, mine)
+
+    norm_copy(half).wait_recv()
+    project(1 - mine)
+
+    def q_copy(delta):
+        return remote(
+            qb.at[half], qb.at[half], q_send.at[delta - 1], q_recv.at[delta - 1], at_half(half - delta)
+        )
+
+    for delta in range(1, halves):
+
+        @pl.when(below(delta))
+        def _():
+            q_copy(delta).start()
+
+    own_block(1 - mine, 1 - mine)
+    own_block(1, 0)
 
     for delta in range(1, halves):
 
         @pl.when(below(delta))
         def _():
             h = half - delta
-            norm_copy(h).wait_recv()
-            project_low(h, 1 - mine)
-            for qi in range(2):
-                scores_of(h, half, h, qi, 2)
-                attend(h, h, qi, 2)
+            relay_spots(h, delta).wait_recv()
+            for d in [0] + order:
+                relay(h, d, delta).wait_recv()
+
+    for delta in range(1, halves):
+
+        @pl.when(below(delta))
+        def _():
+            h = half - delta
+            ingest(h)
+            norm_copy(h).start()
+            for ki in (mine, 1 - mine):
+                if ki is not mine:
+                    norm_copy(h).wait_recv()
+                project_low(h, ki)
+                for qi in range(2):
+                    scores_of(h, half, qi, h, ki)
+                    attend(h, qi, h, ki)
 
     attended = att[...]
     gate_u = gate_sc[...].astype(F32)
@@ -577,7 +588,13 @@
         return (own // bit) % 2, device
 
     all_streams = early + middle + late
-    starts = [[base] for base, _, _ in all_streams]
+    starts = []
+    for base, size, bit_order in all_streams:
+        offsets = [base]
+        for stage in range(stages):
+            side, _ = place_of(*bit_order[stage])
+            offsets.append(offsets[stage] + side * (size >> (stage + 1)))
+        starts.append(offsets)
     landings = []
     landing_at = 0
     for base, size, _ in all_streams:
@@ -633,7 +650,6 @@
             summed = (
                 work[pl.ds(keep, part)].astype(F32) + landing[at : at + part].astype(F32)
             ).astype(BF16)
-            starts[i].append(keep)
             if stage + 1 < stages:
                 work[pl.ds(keep, part)] = summed
                 reduce_copy(i, stage + 1)[0].start()
@@ -677,7 +693,8 @@
                 qb.at[h], qb.at[h], q_send.at[delta - 1], q_recv.at[delta - 1], at_half(half)
             ).wait_recv()
             for qi in range(2):
-                scores_of(h, h, half, qi, 2)
+                for ki in range(2):
+                    scores_of(h, h, qi, half, ki)
 
     def backward(slot, q_half, k_half, qi, keys_to, query_side, key_side):
         qr = slice(qi * block, (qi + 1) * block)
@@ -725,8 +742,10 @@
     clear(filled, late_base)
     reduce_start(middle_ids)
 
-    advance(early_ids, 0)
-    advance(early_ids, 1)
+    @pl.when(above(1))
+    def _():
+        advance(early_ids, 0)
+        advance(early_ids, 1)
 
     for delta in range(1, halves):
 
@@ -769,6 +788,11 @@
         + seq_sc[...].astype(F32)
     )
     layer_ref[...] = jnp.where(present_at(mine), result, 0.0).astype(BF16)
+
+    @pl.when(jnp.logical_not(above(1)))
+    def _():
+        advance(early_ids, 0)
+        advance(early_ids, 1)
 
     for turn in range(2 * stages + 1):
         advance(late_ids, turn)
@@ -871,14 +895,17 @@
     anywhere = pl.BlockSpec(memory_space=pl.ANY)
     smem = pl.BlockSpec(memory_space=pltpu.SMEM)
     dma = pltpu.SemaphoreType.DMA
+    resident = 2 * total <= RESIDENT
+    result = pltpu.VMEM if resident else jax.ShapeDtypeStruct
     layer, full, bias = pl.pallas_call(
         functools.partial(kernel, users, seqs),
         out_shape=(
-            jax.ShapeDtypeStruct((block, model), BF16),
-            jax.ShapeDtypeStruct((2, total, ROWS, LANES), BF16),
-            jax.ShapeDtypeStruct((2, 2, 4 * share), F32),
+            result((block, model), BF16),
+            result((2, total, ROWS, LANES), BF16),
+            result((2, 2, 4 * share), F32),
         ),
-        in_specs=[anywhere, vmem, vmem, smem, smem] + [anywhere] * 4 + [vmem, anywhere, vmem],
+        in_specs=[anywhere, vmem, vmem, smem, pl.BlockSpec(memory_space=pltpu.HBM)]
+        + [anywhere] * 4 + [vmem, anywhere, vmem],
         out_specs=(vmem,) * 3,
         scratch_shapes=[
             pltpu.VMEM((users, cap_pad, model), BF16),
@@ -941,6 +968,8 @@
             dma((stages + 1,)),
             dma((stages + 1,)),
             dma((9,)),
+            pltpu.SMEM(lengths.shape, jnp.int32),
+            dma,
         ],
         compiler_params=pltpu.CompilerParams(
             collective_id=0, has_side_effects=True, vmem_limit_bytes=60000 * 1024
@@ -959,6 +988,9 @@
         out_weight,
         out_bias[None],
     )
+    held = (full, bias, layer)
+    if resident:
+        held = [pltpu.with_memory_space_constraint(array, pltpu.VMEM) for array in held]
     layer_out, grad_pw, grad_pb, grad_ow, grad_ob = pl.pallas_call(
         functools.partial(unpack, bases=[plan[0][0] for plan in plans]),
         out_shape=(
@@ -970,7 +1002,7 @@
         ),
         in_specs=[vmem] * 3,
         out_specs=(vmem,) * 5,
-    )(full, bias, layer)
+    )(*held)
     return layer_out[None], grad_pw, grad_pb[0], grad_ow, grad_ob[0]
 
 

time: 68.7 us -> 62.5 us (0.910)
  Pallas kernels: 67.3 us -> 61 us
    pallas_call x1, Pallas kernels: 64.4 us -> 59.5 us  [on_device(): pl.pallas_call(functools.partial(kernel, users, seqs), out_shape=(result(...]
    pallas_call x1, Pallas kernels: 2.84 us -> 1.5 us  [on_device(): pl.pallas_call(functools.partial(unpack, bases=[plan[0][0] for plan in pl...]
where the time goes in v2:
time: 62.5 us; the launch traced here: 62.3 us
  Pallas kernels  61 us (98%)
  between operations  1.29 us (2%)
    pallas_call x1, Pallas kernels, on_device(): pl.pallas_call(functools.partial(kernel, users, seqs), out_shape=(result(...  59.5 us
    pallas_call x1, Pallas kernels, on_device(): pl.pallas_call(functools.partial(unpack, bases=[plan[0][0] for plan in pl...  1.5 us

profile of v2, /device:TPU:0, one launch (start us, length us, event | category | flops | bytes accessed | tf_op | source)
XLA Modules:
  0.0 62.3 jit_solution(9658799023143513403)
XLA Ops:
  1.3 59.5 %shard_map.155 = (bf16[256,512]{1,0:T(8,128)(2,1)S(1)}, bf16[2,160,16,128]{3,2,1,0:T(8,128)(2,1)S(1)}, f32[2,2,512]{2,1,0:T(2,128)S(1)}) custom-call(bf16[384,512]{1,0:T(8,128)(2,1)} %bitcast.8, s32[1,384]{1,0:T(1,128)} %user_ref.1, s32[1,384]{1,0:T(1,128)} %place_ref.1, s32[1,8]{1,0:T(1,128)} %bitcast.12, s32[1]{0:T(128)S(6)} %copy.17.length_hbm, ...), custom_call_target="tpu_custom_call" | custom-call | tf_op jit(solution)/shard_map/pallas_call | solution.py:900
  60.8 1.5 %shard_map.156 = (bf16[256,512]{1,0:T(8,128)(2,1)}, bf16[512,1024]{1,0:T(8,128)(2,1)}, f32[1,1024]{1,0:T(1,128)}, bf16[256,512]{1,0:T(8,128)(2,1)}, f32[1,512]{1,0:T(1,128)}) custom-call(bf16[2,160,16,128]{3,2,1,0:T(8,128)(2,1)S(1)} %get-tuple-element.13.full, f32[2,2,512]{2,1,0:T(2,128)S(1)} %get-tuple-element.14.bias_ref, ...), custom_call_target="tpu_custom_call" | custom-call | tf_op jit(solution)/shard_map/pallas_call | solution.py:994

commit v3 on v2

--- a/solution.py
+++ b/solution.py
@@ -12,6 +12,7 @@
 LANES = 128
 ROWS = 16
 RESIDENT = 320
+QUAD = (1, 2, 3)
 F32 = jnp.float32
 BF16 = jnp.bfloat16
 
@@ -70,17 +71,15 @@
     for chunks, most, across_first in groups:
         each = -(-chunks // devices)
         if across_first:
-            turn = (far + near)[:3]
-            tail = (far + near)[3:]
+            turn, tail = far + near[:-2], near[-2:]
         else:
-            turn = near[:2]
-            tail = near[2:] + far
+            turn, tail = [], near[:-2] + far + near[-2:]
         streams = []
         for i in range(most):
             share = (each + most - 1 - i) // most
             if share == 0:
                 continue
-            k = i % len(turn)
+            k = i % max(len(turn), 1)
             streams.append((base, share * devices, turn[k:] + turn[:k] + tail))
             base += share * devices
         plans.append(streams)
@@ -91,7 +90,7 @@
     tile = ROWS * LANES
     return (
         (2 * model * share // tile, 2, False),
-        (model * share // tile, 2, False),
+        (model * share // tile, 2, True),
         (2 * model * share // tile, 4, True),
     )
 
@@ -624,6 +623,59 @@
             part,
         )
 
+    def quad_of(i, mask):
+        base, size, bit_order = all_streams[i]
+        (axis_a, bit_a), (axis_b, bit_b) = bit_order[stages - 2 :]
+        place = {"users": me_u, "seq": me_s}
+        side_a, side_b = (place[axis_a] // bit_a) % 2, (place[axis_b] // bit_b) % 2
+        if mask & 2:
+            place[axis_a] = flip(place[axis_a], bit_a)
+            side_a = 1 - side_a
+        if mask & 1:
+            place[axis_b] = flip(place[axis_b], bit_b)
+            side_b = 1 - side_b
+        part = size >> stages
+        theirs = starts[i][stages - 2] + (2 * side_a + side_b) * part
+        return (place["users"], place["seq"]), theirs, part
+
+    def reduce_quad_copy(i, mask):
+        device, theirs, part = quad_of(i, mask)
+        slot = stages - 3 + mask
+        return remote(
+            work.at[pl.ds(theirs, part)],
+            landing.at[pl.ds(landings[i][stages - 2] + (mask - 1) * part, part)],
+            rs_send.at[i, slot],
+            rs_recv.at[i, slot],
+            device,
+        )
+
+    def gather_quad_copy(i, mask):
+        device, _, part = quad_of(i, mask)
+        slot = stages - 3 + mask
+        own = full.at[mine, pl.ds(starts[i][stages], part)]
+        return remote(own, own, ag_send.at[i, slot], ag_recv.at[i, slot], device)
+
+    def reduce_quad(ids):
+        for i in ids:
+            part = all_streams[i][1] >> stages
+            own = pl.ds(starts[i][stages], part)
+            summed = work[own].astype(F32)
+            for mask in QUAD:
+                reduce_quad_copy(i, mask).wait()
+                at = landings[i][stages - 2] + (mask - 1) * part
+                summed = summed + landing[at : at + part].astype(F32)
+            full[mine, own] = summed.astype(BF16)
+            for mask in QUAD:
+                gather_quad_copy(i, mask).start()
+
+    def gather_quad(ids):
+        for i in ids:
+            for mask in QUAD:
+                gather_quad_copy(i, mask).wait()
+            gather_copy(i, stages - 3).start()
+            if stages == 3:
+                core_copy(i, 0).start()
+
     def gather_copy(i, stage):
         base, size, bit_order = all_streams[i]
         _, device = place_of(*bit_order[stage])
@@ -650,14 +702,12 @@
             summed = (
                 work[pl.ds(keep, part)].astype(F32) + landing[at : at + part].astype(F32)
             ).astype(BF16)
-            if stage + 1 < stages:
-                work[pl.ds(keep, part)] = summed
+            work[pl.ds(keep, part)] = summed
+            if stage + 1 < stages - 2:
                 reduce_copy(i, stage + 1)[0].start()
             else:
-                full[mine, pl.ds(keep, part)] = summed
-                gather_copy(i, stage).start()
-                if stage == 0:
-                    core_copy(i, 0).start()
+                for mask in QUAD:
+                    reduce_quad_copy(i, mask).start()
 
     def gather_step(ids, stage):
         for i in ids:
@@ -675,11 +725,15 @@
             core_copy(i, 1).wait()
 
     def advance(ids, turn):
-        if turn < stages:
+        if turn < stages - 2:
             reduce_step(ids, turn)
-        elif turn < 2 * stages:
-            gather_step(ids, 2 * stages - 1 - turn)
-        elif turn == 2 * stages:
+        elif turn == stages - 2:
+            reduce_quad(ids)
+        elif turn == stages - 1:
+            gather_quad(ids)
+        elif turn < 2 * stages - 2:
+            gather_step(ids, 2 * stages - 3 - turn)
+        elif turn == 2 * stages - 2:
             core_finish(ids)
 
     reduce_start(early_ids)
@@ -742,10 +796,7 @@
     clear(filled, late_base)
     reduce_start(middle_ids)
 
-    @pl.when(above(1))
-    def _():
-        advance(early_ids, 0)
-        advance(early_ids, 1)
+    advance(early_ids, 0)
 
     for delta in range(1, halves):
 
@@ -789,12 +840,7 @@
     )
     layer_ref[...] = jnp.where(present_at(mine), result, 0.0).astype(BF16)
 
-    @pl.when(jnp.logical_not(above(1)))
-    def _():
-        advance(early_ids, 0)
-        advance(early_ids, 1)
-
-    for turn in range(2 * stages + 1):
+    for turn in range(2 * stages - 1):
         advance(late_ids, turn)
         if turn < stages:
             bias_step(turn)
@@ -804,7 +850,7 @@
             bias_final = remote(bias_own, bias_own, b_send.at[stages], b_recv.at[stages], partner)
             bias_final.start()
         advance(middle_ids, turn)
-        advance(early_ids, turn + 2)
+        advance(early_ids, turn + 1)
 
     bias_final.wait()
     for d in order:
@@ -959,10 +1005,10 @@
             dma((others,)),
             dma((others, 2)),
             dma((others, 2)),
-            dma((count, stages)),
-            dma((count, stages)),
-            dma((count, stages)),
-            dma((count, stages)),
+            dma((count, stages + 1)),
+            dma((count, stages + 1)),
+            dma((count, stages + 1)),
+            dma((count, stages + 1)),
             dma((count, 2)),
             dma((count, 2)),
             dma((stages + 1,)),

time: 62.5 us -> 58.2 us (0.931)
  Pallas kernels: 61 us -> 56.7 us
    pallas_call x1, Pallas kernels: 59.5 us -> 55.2 us  [on_device(): pl.pallas_call(functools.partial(kernel, users, seqs), out_shape=(result(...]
where the time goes in v3:
time: 58.2 us; the launch traced here: 58 us
  Pallas kernels  56.7 us (97%)
  between operations  1.29 us (2%)
    pallas_call x1, Pallas kernels, on_device(): pl.pallas_call(functools.partial(kernel, users, seqs), out_shape=(result(...  55.2 us
    pallas_call x1, Pallas kernels, on_device(): pl.pallas_call(functools.partial(unpack, bases=[plan[0][0] for plan in pl...  1.5 us

profile of v3, /device:TPU:0, one launch (start us, length us, event | category | flops | bytes accessed | tf_op | source)
XLA Modules:
  0.0 58.0 jit_solution(15207925182527279632)
XLA Ops:
  1.3 55.2 %shard_map.155 = (bf16[256,512]{1,0:T(8,128)(2,1)S(1)}, bf16[2,160,16,128]{3,2,1,0:T(8,128)(2,1)S(1)}, f32[2,2,512]{2,1,0:T(2,128)S(1)}) custom-call(bf16[384,512]{1,0:T(8,128)(2,1)} %bitcast.8, s32[1,384]{1,0:T(1,128)} %user_ref.1, s32[1,384]{1,0:T(1,128)} %place_ref.1, s32[1,8]{1,0:T(1,128)} %bitcast.12, s32[1]{0:T(128)S(6)} %copy.17.length_hbm, ...), custom_call_target="tpu_custom_call" | custom-call | tf_op jit(solution)/shard_map/pallas_call | solution.py:946
  56.5 1.5 %shard_map.156 = (bf16[256,512]{1,0:T(8,128)(2,1)}, bf16[512,1024]{1,0:T(8,128)(2,1)}, f32[1,1024]{1,0:T(1,128)}, bf16[256,512]{1,0:T(8,128)(2,1)}, f32[1,512]{1,0:T(1,128)}) custom-call(bf16[2,160,16,128]{3,2,1,0:T(8,128)(2,1)S(1)} %get-tuple-element.13.full, f32[2,2,512]{2,1,0:T(2,128)S(1)} %get-tuple-element.14.bias_ref, ...), custom_call_target="tpu_custom_call" | custom-call | tf_op jit(solution)/shard_map/pallas_call | solution.py:1040
